TPU v7x, 256 devices: a whole 4x4x8 slice. The times are simulated.
256 devices in a mesh: wide: 32 (over x, y, core), narrow: 8 (over z).
Axes of the slice: x: 4, y: 4, z: 8, core: 2. Of those that a mesh axis runs over, the one named last changes fastest.
Arguments:
- residual: bfloat16 [8192, 4608], P('wide'), may hold values from -6 to 6
- pre_gain: bfloat16 [4608], replicated, may hold values from 0.5 to 1.5
- query_weight: bfloat16 [4608, 4096], P('wide', 'narrow'), may hold values from -0.09375 to 0.09375
- key_weight: bfloat16 [4608, 2048], P('wide', 'narrow'), may hold values from -0.09375 to 0.09375
- value_weight: bfloat16 [4608, 2048], P('wide', 'narrow'), may hold values from -0.09375 to 0.09375
- output_weight: bfloat16 [4096, 4608], P('narrow', 'wide'), may hold values from -1 to 1
- adapter_down: bfloat16 [4608, 768], P('wide', 'narrow'), may hold values from -0.09375 to 0.09375
- adapter_up_query: bfloat16 [256, 4096], P(None, 'narrow'), may hold values from -1.5 to 1.5
- adapter_up_key: bfloat16 [256, 2048], P(None, 'narrow'), may hold values from -1.5 to 1.5
- adapter_up_value: bfloat16 [256, 2048], P(None, 'narrow'), may hold values from -1.5 to 1.5
- adapter_down_out: bfloat16 [4096, 256], P('narrow'), may hold values from -0.09375 to 0.09375
- adapter_up_out: bfloat16 [256, 4608], P(None, 'narrow'), may hold values from -1.5 to 1.5
- post_gain: bfloat16 [4608], P('narrow'), may hold values from 0.5 to 1.5
- sink_logits: float32 [32], P('narrow'), may hold values from -1 to 130
- prompt_lengths: int32 [4], replicated, may hold values from 1 to 4096, 8192 in all
- prompt_adapters: int32 [4], replicated, may hold values from 0 to 15
Outputs:
- layer_out: bfloat16 [8192, 4608], P('wide', 'narrow')
All inputs are finite; a program needn't handle non-finite values.
Results may differ from a plain program's by a relative error of at most 0.022.
Values may be sent and summed in bfloat16 or wider, within the bound.
A program may use at most 128 MiB of HBM per device.

v0:
```python
import jax
import jax.numpy as jnp
from jax import lax
from jax.sharding import PartitionSpec as P

HEAD_DIM = 128
ADAPTERS = 16


epsilon = 1e-06
adapter_scale = 0.5
rotary_base = 10000.0
score_scale = 1.0 / 12.0


def token_layout(prompt_lengths, count, first):
    ends = jnp.cumsum(prompt_lengths, dtype=jnp.int32)
    starts = ends - prompt_lengths
    places = first + jnp.arange(count, dtype=jnp.int32)
    member = jnp.logical_and(
        places[:, None] >= starts[None, :], places[:, None] < ends[None, :]
    ).astype(jnp.int32)
    labels = jnp.arange(prompt_lengths.shape[0], dtype=jnp.int32)
    prompt = jnp.sum(member * labels[None, :], axis=1)
    position = places - jnp.sum(member * starts[None, :], axis=1)
    return (member, prompt, position)


def rotate(values, position):
    half = values.shape[-1] // 2
    exponent = jnp.arange(half, dtype=jnp.float32) * (2.0 / values.shape[-1])
    frequency = jnp.power(jnp.float32(rotary_base), -exponent)
    angle = position.astype(jnp.float32)[:, None] * frequency[None, :]
    cosine = jnp.cos(angle)[:, None, :]
    sine = jnp.sin(angle)[:, None, :]
    first_half = values[..., :half]
    second_half = values[..., half:]
    return jnp.concatenate(
        [first_half * cosine - second_half * sine, second_half * cosine + first_half * sine],
        axis=-1,
    )


def select_codes(codes, adapter, projections, adapters):
    count = codes.shape[0]
    width = codes.shape[1] // (adapters * projections)
    shaped = codes.reshape(count, adapters, projections, width)
    onehot = (adapter[:, None] == jnp.arange(adapters, dtype=jnp.int32)[None, :]).astype(
        codes.dtype
    )
    kept = shaped * onehot[:, :, None, None]
    return [kept[:, :, slot, :].reshape(count, adapters * width) for slot in range(projections)]


def add_adapter(partial_out, adapter_cols, offset, own_width):
    current = lax.dynamic_slice_in_dim(partial_out, offset, own_width, 1)
    return lax.dynamic_update_slice_in_dim(partial_out, current + adapter_cols, offset, 1)


def per_device(
    residual,
    pre_gain,
    query_weight,
    key_weight,
    value_weight,
    output_weight,
    adapter_down,
    adapter_up_query,
    adapter_up_key,
    adapter_up_value,
    adapter_down_out,
    adapter_up_out,
    post_gain,
    sink_logits,
    prompt_lengths,
    prompt_adapters,
):
    tok_rows = residual.shape[0]
    first = lax.axis_index("wide") * tok_rows
    member, prompt, position = token_layout(prompt_lengths, tok_rows, first)
    adapter = jnp.sum(member * prompt_adapters[None, :], axis=1)
    stream = residual.astype(jnp.float32)
    scale_rows = lax.rsqrt(jnp.mean(stream * stream, axis=1, keepdims=True) + epsilon)
    normed = (stream * scale_rows * pre_gain.astype(jnp.float32)[None, :]).astype(jnp.bfloat16)
    query_cols = query_weight.shape[1]
    key_cols = key_weight.shape[1]
    pieces = (
        lax.all_gather(query_weight, "wide", axis=0, tiled=True),
        lax.all_gather(key_weight, "wide", axis=0, tiled=True),
        lax.all_gather(value_weight, "wide", axis=0, tiled=True),
        lax.all_gather(adapter_down, "wide", axis=0, tiled=True),
    )
    query_part, key_part, value_part, code_part = tuple(
        (jnp.dot(normed, piece, preferred_element_type=jnp.float32) for piece in pieces)
    )
    codes = lax.all_gather(code_part.astype(jnp.bfloat16), "narrow", axis=1, tiled=True)
    chosen = select_codes(codes, adapter, 3, ADAPTERS)
    query = query_part + adapter_scale * jnp.dot(
        chosen[0], adapter_up_query, preferred_element_type=jnp.float32
    )
    key = key_part + adapter_scale * jnp.dot(
        chosen[1], adapter_up_key, preferred_element_type=jnp.float32
    )
    value = value_part + adapter_scale * jnp.dot(
        chosen[2], adapter_up_value, preferred_element_type=jnp.float32
    )
    local_heads = query_cols // HEAD_DIM
    local_kv = key_cols // HEAD_DIM
    group = local_heads // local_kv
    queries = (
        rotate(query.reshape(tok_rows, local_heads, HEAD_DIM), position)
        .astype(jnp.bfloat16)
        .reshape(tok_rows, local_kv, group, HEAD_DIM)
    )
    keys = rotate(key.reshape(tok_rows, local_kv, HEAD_DIM), position).astype(jnp.bfloat16)
    values = value.astype(jnp.bfloat16).reshape(tok_rows, local_kv, HEAD_DIM)
    sinks = sink_logits.reshape(local_kv, group)
    own_places = first + jnp.arange(tok_rows, dtype=jnp.int32)
    start_top = jnp.broadcast_to(sinks[None, :, :], (tok_rows, local_kv, group))
    start_total = jnp.ones((tok_rows, local_kv, group), jnp.float32)
    start_sum = jnp.zeros((tok_rows, local_kv, group, HEAD_DIM), jnp.float32)
    top = start_top
    total = start_total
    summed_values = start_sum
    piece_keys = lax.all_gather(keys, "wide", axis=0, tiled=True)
    piece_values = lax.all_gather(values, "wide", axis=0, tiled=True)
    count = piece_keys.shape[0]
    unused, key_prompt, unused_position = token_layout(prompt_lengths, count, jnp.int32(0))
    key_places = jnp.arange(count, dtype=jnp.int32)
    allowed = jnp.logical_and(
        prompt[:, None] == key_prompt[None, :], own_places[:, None] >= key_places[None, :]
    )[:, None, None, :]
    scores = (
        jnp.einsum("qgjd,kgd->qgjk", queries, piece_keys, preferred_element_type=jnp.float32)
        * score_scale
    )
    scores = jnp.where(allowed, scores, -1e30)
    fresh = jnp.maximum(top, jnp.max(scores, axis=-1))
    factor = jnp.exp(top - fresh)
    weights = jnp.where(allowed, jnp.exp(scores - fresh[..., None]), 0.0)
    total = total * factor + jnp.sum(weights, axis=-1)
    update = jnp.einsum(
        "qgjk,kgd->qgjd",
        weights.astype(jnp.bfloat16),
        piece_values,
        preferred_element_type=jnp.float32,
    )
    top, total, summed_values = (fresh, total, summed_values * factor[..., None] + update)
    attended = (
        (summed_values / total[..., None])
        .reshape(tok_rows, local_heads * HEAD_DIM)
        .astype(jnp.bfloat16)
    )
    code_terms = jnp.dot(attended, adapter_down_out, preferred_element_type=jnp.float32)
    codes_out = lax.psum(code_terms.astype(jnp.bfloat16), "narrow")
    chosen_out = select_codes(codes_out, adapter, 1, ADAPTERS)[0]
    adapter_cols = adapter_scale * jnp.dot(
        chosen_out, adapter_up_out, preferred_element_type=jnp.float32
    )
    own_width = adapter_up_out.shape[1]
    offset = lax.axis_index("narrow") * own_width
    partial_out = jnp.dot(
        attended,
        lax.all_gather(output_weight, "wide", axis=1, tiled=True),
        preferred_element_type=jnp.float32,
    )
    partial_out = add_adapter(partial_out, adapter_cols, offset, own_width)
    whole = lax.psum(partial_out.astype(jnp.bfloat16), "narrow").astype(jnp.float32)
    mean_square = jnp.mean(whole * whole, axis=1)
    projected = lax.dynamic_slice_in_dim(whole, offset, own_width, 1)
    factor_rows = lax.rsqrt(mean_square + epsilon)
    own_stream = lax.dynamic_slice_in_dim(stream, offset, own_width, 1)
    mixed = own_stream + projected * factor_rows[:, None] * post_gain.astype(jnp.float32)[None, :]
    return mixed.astype(jnp.bfloat16)


def solution(mesh):
    return jax.shard_map(
        per_device,
        mesh=mesh,
        in_specs=(
            P("wide", None),
            P(),
            P("wide", "narrow"),
            P("wide", "narrow"),
            P("wide", "narrow"),
            P("narrow", "wide"),
            P("wide", "narrow"),
            P(None, "narrow"),
            P(None, "narrow"),
            P(None, "narrow"),
            P("narrow", None),
            P(None, "narrow"),
            P("narrow"),
            P("narrow"),
            P(),
            P(),
        ),
        out_specs=P("wide", "narrow"),
        check_vma=False,
    )
```

profile of v0, /device:TPU:1, one launch (start us, length us, event | category | flops | bytes accessed | tf_op | source)
XLA Modules:
  0.0 506.7 jit_solution(2858889382094123757)
XLA Ops:
  6.5 0.7 all-gather.7.cloned.1.call-update
  7.3 0.7 all-gather.13.cloned.1.call-update
  8.1 0.7 all-gather.11.cloned.1.call-update
  8.8 0.7 convert_element_type.59
  9.5 0.8 reduce-window.8
  10.3 0.7 bitcast_subtract_fusion
  11.0 0.7 select_reduce_fusion.3
  11.8 27.4 %all_gather.25 = bf16[4608,96]{1,0:T(8,128)(2,1)S(1)} all-gather(bf16[144,96]{1,0:T(8,128)(2,1)} %param.22), channel_id=1, replica_groups=mesh['wide'=32,'narrow'=8] {'wide'}, dimensions={0}, use_global_device_ids=true | all-gather | bytes 912384 | tf_op jit(solution)/shard_map/all_gather | solution.py:91
  39.2 2.4 multiply_reduce_fusion.1
  41.6 2.7 convolution_convert_fusion.1
  44.2 23.0 %all_gather.26 = bf16[256,768]{0,1:T(8,128)(2,1)S(1)} all-gather(bf16[256,96]{0,1:T(8,128)(2,1)S(1)} %convolution_convert_fusion.1), channel_id=1, replica_groups=mesh['wide'=32,'narrow'=8] {'narrow'}, dimensions={1}, use_global_device_ids=true | all-gather | bytes 442368 | tf_op jit(solution)/shard_map/all_gather | solution.py:96
  67.3 0.5 multiply_cosine_fusion
  67.8 0.7 fusion.50
  68.6 2.9 fusion.49
  71.5 0.2 fusion.23
  71.7 0.7 fusion.51
  72.6 1.0 copy.45
  73.7 0.8 pad_maximum_fusion
  74.5 39.3 %all-gather.13.cloned.1.call-done = bf16[4608,256]{1,0:T(8,128)(2,1)} async-done(((bf16[144,256]{1,0:T(8,128)(2,1)}), bf16[4608,256]{1,0:T(8,128)(2,1)}) %all-gather.13.cloned.1.call-update) | async-done | bytes 2359312 | tf_op jit(solution)/shard_map/all_gather | solution.py:90
  113.8 2.9 fusion.47
  116.8 0.9 fusion.24
  117.7 0.5 all-gather.17.cloned.1.call-update
  118.8 0.8 copy.37
  119.6 4.6 fusion.6
  124.2 43.3 %all-gather.11.cloned.1.call-done = bf16[4608,512]{1,0:T(8,128)(2,1)} async-done(((bf16[144,512]{1,0:T(8,128)(2,1)}), bf16[4608,512]{1,0:T(8,128)(2,1)}) %all-gather.11.cloned.1.call-update) | async-done | bytes 4718608 | tf_op jit(solution)/shard_map/all_gather | solution.py:88
  167.5 3.7 fusion.48
  171.3 1.0 fusion.11
  172.3 1.2 reshape.200
  173.5 0.5 subtract_convert_fusion
  174.1 46.4 %all-gather.9.cloned.1.call-done = bf16[8192,2,128]{2,0,1:T(8,128)(2,1)} async-done(((bf16[256,2,128]{2,0,1:T(8,128)(2,1)}), bf16[8192,2,128]{2,0,1:T(8,128)(2,1)}) %all-gather.9.cloned.1.call-update) | async-done | bytes 4194320 | tf_op jit(solution)/shard_map/all_gather | solution.py:125
  220.5 16.1 %fusion = (f32[256,2,2]{0,2,1:T(2,128)S(1)}, f32[2,8192,256,2]{2,1,3,0:T(8,128)}) fusion(pred[256,8192]{0,1:T(8,128)(4,1)} %fusion.6, bf16[256,2,2,64]{3,0,2,1:T(8,128)(2,1)S(1)} %bitcast.85, bf16[256,2,2,64]{3,0,2,1:T(8,128)(2,1)S(1)} %bitcast.84, bf16[8192,2,128]{2,0,1:T(8,128)(2,1)} %all-gather.9.cloned.1.call-done), kind=kOutput, calls=%fused_computation.2 | convolution fusion | flops 2173172736 | bytes 40112128 | tf_op jit(solution)/shard_map/qgjd,kgd->qgjk/dot_general | solution.py:134
  236.7 15.0 %fusion.1 = f32[256,2,2]{0,2,1:T(2,128)S(1)} fusion(f32[2,8192,256,2]{2,1,3,0:T(8,128)} %get-tuple-element.22, f32[256,2,2]{0,2,1:T(2,128)S(1)} %broadcast_maximum_fusion, pred[256,8192]{0,1:T(8,128)(4,1)S(1)} %copy-done.2), kind=kLoop, calls=%fused_computation.3 | loop fusion | flops 41942016 | bytes 35659776 | tf_op jit(solution)/shard_map/reduce_sum | solution.py:141
  251.8 24.1 %all-gather.15.cloned.1.call-done = bf16[8192,2,128]{0,2,1:T(8,128)(2,1)} async-done(((bf16[256,2,128]{0,2,1:T(8,128)(2,1)}), bf16[8192,2,128]{0,2,1:T(8,128)(2,1)}) %all-gather.15.cloned.1.call-update) | async-done | bytes 4194320 | tf_op jit(solution)/shard_map/all_gather | solution.py:126
  275.9 15.9 %fusion.30 = bf16[256,2,2,128]{0,3,2,1:T(8,128)(2,1)S(1)} fusion(f32[2,8192,256,2]{2,1,3,0:T(8,128)} %get-tuple-element.22, f32[256,2,2]{0,2,1:T(2,128)S(1)} %broadcast_maximum_fusion, pred[256,8192]{0,1:T(8,128)(4,1)} %fusion.6, bf16[8192,2,128]{0,2,1:T(8,128)(2,1)} %all-gather.15.cloned.1.call-done, f32[256,2,2]{0,2,1:T(2,128)S(1)} %get-tuple-element.18, ...), kind=kOutput, calls=%fused_computation.29 | convolution fusion | flops 2189819904 | bytes 40120320 | tf_op jit(solution)/shard_map/qgjk,kgd->qgjd/dot_general | solution.py:142
  291.9 0.9 convolution_convert_fusion
  292.8 0.3 all-reduce.5.cloned.1.call-start
  293.1 36.5 %all-gather.17.cloned.1.call-done = bf16[512,4608]{0,1:T(8,128)(2,1)} async-done(((bf16[512,144]{0,1:T(8,128)(2,1)}), bf16[512,4608]{0,1:T(8,128)(2,1)}) %all-gather.17.cloned.1.call-update) | async-done | bytes 4718608 | tf_op jit(solution)/shard_map/all_gather | solution.py:164
  329.6 5.9 %fusion.52 = f32[256,4608]{1,0:T(8,128)} fusion(bf16[256,512]{0,1:T(8,128)(2,1)S(1)} %bitcast.77, bf16[512,4608]{0,1:T(8,128)(2,1)} %all-gather.17.cloned.1.call-done), kind=kOutput, calls=%fused_computation.72 | convolution fusion | flops 1207959552 | bytes 9699328 | tf_op jit(solution)/shard_map/dot_general | solution.py:162
  335.5 62.9 %all-reduce.3.cloned.1.call-done = bf16[256,256]{1,0:T(8,128)(2,1)} async-done(((bf16[256,256]{1,0:T(8,128)(2,1)}), bf16[256,256]{1,0:T(8,128)(2,1)}) %all-reduce.3.cloned.1.call-update) | async-done | bytes 131088 | tf_op jit(solution)/shard_map/psum | solution.py:155
  398.4 1.5 fusion.10
  399.9 4.5 dynamic_update_slice.3
  404.5 4.0 convert_element_type.69
  408.5 2.7 convert_element_type.58
  411.2 81.8 %all-reduce.5.cloned.1.call-done = bf16[256,4608]{1,0:T(8,128)(2,1)} async-done(((bf16[256,4608]{1,0:T(8,128)(2,1)}), bf16[256,4608]{1,0:T(8,128)(2,1)}) %all-reduce.5.cloned.1.call-update) | async-done | bytes 2359312 | tf_op jit(solution)/shard_map/psum | solution.py:168
  493.0 2.2 multiply_reduce_fusion
  495.2 2.2 convert_element_type.70
  497.4 1.6 add_convert_fusion
  499.0 0.9 copy.39
  (53 shorter events, 1.3 us)
Async XLA Ops:
  6.5 391.9 %copy-start = (bf16[256,576]{0,1:T(8,128)(2,1)S(1)}, bf16[256,576]{0,1:T(8,128)(2,1)}, u32[]{:S(2)}) copy-start(bf16[256,576]{0,1:T(8,128)(2,1)} %param.27) | copy-start | bytes 884740
  6.5 62.0 %all-gather.7.cloned.1.call-start = ((), (), s32[]{:S(2)}) async-start(), calls=%async_computation | async-start | bytes 2433024 | tf_op jit(solution)/shard_map/all_gather | solution.py:89
  7.3 106.6 %all-gather.13.cloned.1.call-start = ((), (), s32[]{:S(2)}) async-start(), calls=%async_computation.3 | async-start | bytes 2433024 | tf_op jit(solution)/shard_map/all_gather | solution.py:90
  8.0 159.5 %all-gather.11.cloned.1.call-start = ((), (), s32[]{:S(2)}) async-start(), calls=%async_computation.2 | async-start | bytes 4866048 | tf_op jit(solution)/shard_map/all_gather | solution.py:88
  8.7 211.8 %all-gather.9.cloned.1.call-start = ((), (), s32[]{:S(2)}) async-start(), calls=%async_computation.1 | async-start | bytes 4325376 | tf_op jit(solution)/shard_map/all_gather | solution.py:125
  39.2 29.4 %copy-start.1 = (bf16[256,4608]{1,0:T(8,128)(2,1)S(1)}, bf16[256,4608]{1,0:T(8,128)(2,1)}, u32[]{:S(2)}) copy-start(bf16[256,4608]{1,0:T(8,128)(2,1)} %param.16) | copy-start | bytes 7077892
  44.2 27.3 %copy-start.9 = (bf16[256,256]{1,0:T(8,128)(2,1)S(1)}, bf16[256,256]{1,0:T(8,128)(2,1)}, u32[]{:S(2)}) copy-start(bf16[256,256]{1,0:T(8,128)(2,1)} %param.24) | copy-start | bytes 393220
  72.5 46.2 %copy-start.11 = (f32[4]{0:T(128)S(1)}, f32[4]{0:T(128)}, u32[]{:S(2)}) copy-start(f32[4]{0:T(128)} %param.29) | copy-start | bytes 52
  73.7 43.1 %copy-start.4 = (bf16[256,16,1,16]{0,3,2,1:T(8,128)(2,1)S(1)}, bf16[256,16,1,16]{0,3,2,1:T(8,128)(2,1)}, u32[]{:S(2)}) copy-start(bf16[256,16,1,16]{0,3,2,1:T(8,128)(2,1)} %get-tuple-element.12) | copy-start | bytes 393220
  73.7 43.1 %copy-start.8 = (bf16[256,256]{1,0:T(8,128)(2,1)S(1)}, bf16[256,256]{1,0:T(8,128)(2,1)}, u32[]{:S(2)}) copy-start(bf16[256,256]{1,0:T(8,128)(2,1)} %param.25) | copy-start | bytes 393220
  74.5 201.4 %all-gather.15.cloned.1.call-start = ((), (), s32[]{:S(2)}) async-start(), calls=%async_computation.4 | async-start | bytes 4325376 | tf_op jit(solution)/shard_map/all_gather | solution.py:126
  117.7 211.9 %all-gather.17.cloned.1.call-start = ((), (), s32[]{:S(2)}) async-start(), calls=%async_computation.5 | async-start | bytes 4866048 | tf_op jit(solution)/shard_map/all_gather | solution.py:164
  118.3 280.1 %all-reduce.3.cloned.1.call-start = ((), (), s32[]{:S(2)}) async-start(), calls=%async_computation.6 | async-start | bytes 262144 | tf_op jit(solution)/shard_map/psum | solution.py:155
  124.2 47.1 %copy-start.5 = (bf16[256,16,1,16]{0,3,2,1:T(8,128)(2,1)S(1)}, bf16[256,16,1,16]{0,3,2,1:T(8,128)(2,1)}, u32[]{:S(2)}) copy-start(bf16[256,16,1,16]{0,3,2,1:T(8,128)(2,1)} %get-tuple-element.13) | copy-start | bytes 393220
  124.2 47.1 %copy-start.7 = (bf16[256,512]{1,0:T(8,128)(2,1)S(1)}, bf16[256,512]{1,0:T(8,128)(2,1)}, u32[]{:S(2)}) copy-start(bf16[256,512]{1,0:T(8,128)(2,1)} %param.23) | copy-start | bytes 786436
  220.5 16.2 %copy-start.2 = (pred[256,8192]{0,1:T(8,128)(4,1)S(1)}, pred[256,8192]{0,1:T(8,128)(4,1)}, u32[]{:S(2)}) copy-start(pred[256,8192]{0,1:T(8,128)(4,1)} %fusion.6) | copy-start | bytes 6291460
  275.9 15.9 %copy-start.6 = (bf16[512,256]{1,0:T(8,128)(2,1)S(1)}, bf16[512,256]{1,0:T(8,128)(2,1)}, u32[]{:S(2)}) copy-start(bf16[512,256]{1,0:T(8,128)(2,1)} %param.26) | copy-start | bytes 786436
  292.8 105.6 %copy-start.3 = (bf16[256,256]{1,0:T(8,128)(2,1)S(1)}, bf16[256,256]{1,0:T(8,128)(2,1)}, u32[]{:S(2)}) copy-start(bf16[256,256]{1,0:T(8,128)(2,1)} %copy.37) | copy-start | bytes 393220
  292.8 200.1 %all-reduce.5.cloned.1.call-start = ((), (), s32[]{:S(2)}) async-start(), calls=%async_computation.7 | async-start | bytes 4718592 | tf_op jit(solution)/shard_map/psum | solution.py:168
  408.5 2.7 copy-start.10
Sparse Core Ops, SparseCore 0:
  9.9 53.0 all-gather.6
  65.5 48.2 all-gather.12
  116.4 51.0 all-gather.10
  170.0 50.4 all-gather.8
  222.8 53.0 all-gather.14
  278.3 51.2 all-gather.16
  331.9 66.4 all-reduce.2
  408.6 84.3 all-reduce.4
where the time goes:
time: 510 us; the launch traced here: 507 us
  waiting for transfers between devices  337 us (66%)
  matrix products  54.8 us (11%)
  blocking collectives  50.4 us (10%)
  other arithmetic  40 us (8%)
  between operations  13.8 us (3%)
  local copies, waits for them, and re-layouts  10.1 us (2%)
    psum x1, waiting for transfers between devices, per_device(): lax.psum(partial_out.astype(jnp.bfloat16), 'narrow').astype(jnp.float32)  81.8 us
    psum x1, waiting for transfers between devices, per_device(): codes_out = lax.psum(code_terms.astype(jnp.bfloat16), 'narrow')  62.9 us
    all_gather x1, waiting for transfers between devices, per_device(): piece_keys = lax.all_gather(keys, 'wide', axis=0, tiled=True)  46.4 us
    all_gather x1, waiting for transfers between devices, per_device(): lax.all_gather(query_weight, 'wide', axis=0, tiled=True)  43.3 us
    all_gather x1, waiting for transfers between devices, per_device(): lax.all_gather(value_weight, 'wide', axis=0, tiled=True)  39.3 us
    all_gather x1, waiting for transfers between devices, per_device(): lax.all_gather(output_weight, 'wide', axis=1, tiled=True)  36.5 us
    all_gather x1, blocking collectives, per_device(): lax.all_gather(adapter_down, 'wide', axis=0, tiled=True)  27.4 us
    all_gather x1, waiting for transfers between devices, per_device(): piece_values = lax.all_gather(values, 'wide', axis=0, tiled=True)  24.1 us
  transfers between devices with their start and end apart: 8, of which 7 were waited for; matrix products, arithmetic and copies ran while one was open for 17% of the time, Pallas kernels for 0%

commit v1 on v0

v1 whole, which is shorter than its diff:
```python
import functools

import jax
import jax.numpy as jnp
import numpy as np
from jax import lax
from jax.experimental import pallas as pl
from jax.experimental.pallas import tpu as pltpu
from jax.sharding import PartitionSpec as P

MESH = pl.DeviceIdType.MESH
HEAD = 128
ADAPTERS = 16
RANK = 16
D = 4608
SIDE = 4
CHIPS = 16
PLANES = 8
ROWS = D // (2 * CHIPS)
EPS = 1e-06
SCALE = 0.5
SCORE = 1.0 / 12.0
F32 = jnp.float32
BF16 = jnp.bfloat16


def dot(a, b, ca, cb):
    return lax.dot_general(a, b, (((ca,), (cb,)), ((), ())), preferred_element_type=F32)


class Place:
    def __init__(self):
        wide = lax.axis_index("wide")
        self.plane = lax.axis_index("narrow")
        self.core = lax.rem(wide, 2)
        self.chip = wide // 2
        self.x = self.chip // SIDE
        self.y = lax.rem(self.chip, SIDE)
        self.wide = wide

    def chip_at(self, dx, dy):
        return lax.rem(self.x + dx, SIDE) * SIDE + lax.rem(self.y + dy, SIDE)

    def dev(self, dx, dy, core):
        return (self.chip_at(dx, dy) * 2 + core, self.plane)

    def other_plane(self, dz, core=None):
        core = self.core if core is None else core
        return (self.chip * 2 + core, lax.rem(self.plane + dz, PLANES))


def enter(peers):
    barrier = pltpu.get_barrier_semaphore()
    for peer in peers:
        pl.semaphore_signal(barrier, inc=1, device_id=peer, device_id_type=MESH)
    pl.semaphore_wait(barrier, len(peers))


def plane_peers(me):
    peers = [me.dev(0, 0, 1 - me.core)]
    for dx, dy in ((1, 0), (3, 0), (0, 1), (0, 3)):
        peers += [me.dev(dx, dy, 0), me.dev(dx, dy, 1)]
    return peers


def landed(ref, sem):
    pltpu.make_async_copy(ref, ref, sem).wait()


class Part:
    def __init__(self, me, order, unit, send, recv):
        self.me, self.order, self.unit, self.send, self.recv = me, order, unit, send, recv
        self.sent = []

    def rel(self, f, g):
        return (f, g) if self.order == "xy" else (g, f)

    def at(self, f, g):
        return self.unit(self.me.chip_at(*self.rel(f, g)))

    def target(self, f, g, core):
        return self.me.dev(*self.rel(f, g), core)

    def push(self, src, dst, sem, device):
        copy = pltpu.make_async_remote_copy(
            src_ref=src,
            dst_ref=dst,
            send_sem=self.send.at[len(self.sent)],
            recv_sem=sem,
            device_id=device,
            device_id_type=MESH,
        )
        copy.start()
        self.sent.append(copy)

    def label(self, f, g):
        return self.recv.at[f * 4 + g]

    def single(self, f, s):
        return self.recv.at[16 + f * 2 + s]

    def start_pairs(self, pieces):
        me = self.me
        mine = self.unit(me.chip)
        for d in (1, 3):
            for core in (me.core, 1 - me.core):
                for src, sub in pieces(core):
                    self.push(src, sub(mine, me.core), self.single(4 - d, me.core), self.target(d, 0, core))
        for src, sub in pieces(1 - me.core):
            self.push(src, sub(mine, me.core), self.single(0, me.core), self.target(0, 0, 1 - me.core))
        for n, (src, sub) in enumerate(pieces(me.core)):
            pltpu.make_async_copy(src, sub(mine, me.core), self.single(0, me.core)).start()

    def start_own(self, src, dst):
        self.own = src
        for d in (1, 3):
            self.push(src, dst, self.label(4 - d, 0), self.target(d, 0, self.me.core))

    def far(self):
        return 3 - 2 * self.me.core, 1 + 2 * self.me.core

    def spread(self, f, src=None):
        unit = self.at(f, 0)
        for d in (1, 3):
            self.push(unit if src is None else src, unit, self.label(f, 4 - d), self.target(0, d, self.me.core))

    def second_pairs(self):
        landed(self.at(0, 0).at[0], self.single(0, 0))
        landed(self.at(0, 0).at[1], self.single(0, 1))
        self.spread(0)
        for f in (1, 3):
            for s in (0, 1):
                landed(self.at(f, 0).at[s], self.single(f, s))
        self.after_first()

    def second_own(self):
        self.spread(0, self.own)
        for f in (1, 3):
            landed(self.at(f, 0), self.label(f, 0))
        self.after_first()

    def after_first(self):
        source, step = self.far()
        unit = self.at(source, 0)
        self.push(unit, unit, self.label(2, 0), self.target(step, 0, self.me.core))
        for f in (1, 3):
            self.spread(f)

    def third(self):
        landed(self.at(2, 0), self.label(2, 0))
        self.spread(2)

    def fourth(self, fs=(0, 1, 3, 2)):
        source, step = self.far()
        for f in fs:
            for g in (1, 3):
                landed(self.at(f, g), self.label(f, g))
            unit = self.at(f, source)
            self.push(unit, unit, self.label(f, 2), self.target(0, step, self.me.core))

    def last(self, f):
        landed(self.at(f, 2), self.label(f, 2))

    def finish(self):
        for copy in self.sent:
            copy.wait_send()


def token_facts(lengths, places, adapters=None):
    start = jnp.zeros_like(places)
    adapter = jnp.zeros_like(places)
    begin = jnp.int32(0)
    for p in range(4):
        end = begin + lengths[p]
        member = jnp.logical_and(places >= begin, places < end)
        start = jnp.where(member, begin, start)
        if adapters is not None:
            adapter = jnp.where(member, adapters[p], adapter)
        begin = end
    return start, adapter


def choose(codes, adapter):
    tokens = codes.shape[1]
    spread = jnp.broadcast_to(codes[None], (ADAPTERS, RANK, tokens)).reshape(ADAPTERS * RANK, tokens)
    row = lax.broadcasted_iota(jnp.int32, (ADAPTERS * RANK, tokens), 0) // RANK
    return jnp.where(row == adapter, spread, 0.0).astype(BF16)


def project_kernel(
    lengths, adapters, residual, gain, qw, kw, vw, dn, upq, upk, upv, freq,
    q_out, k_out, v_out,
    other, normed, wq, wkv, down, qacc, kvacc, mixed, mixed_in, code_send, codes,
    send, recv, csend, crecv, rsem,
):
    me = Place()
    c = me.core
    half = residual.shape[0]
    down[...] = jnp.zeros_like(down)
    zpeers = []
    for dz in range(1, PLANES):
        zpeers += [me.other_plane(dz, 0), me.other_plane(dz, 1)]
    enter(plane_peers(me) + zpeers)

    dpart = Part(me, "xy", lambda j: down.at[j, c], send.at[0], recv.at[0])
    qpart = Part(me, "xy", lambda j: wq.at[j], send.at[1], recv.at[1])
    kvpart = Part(me, "yx", lambda j: wkv.at[j], send.at[2], recv.at[2])

    def q_pieces(core):
        cols = pl.ds(pl.multiple_of(core * 256, 256), 256)
        return [(qw.at[:, cols], lambda unit, s: unit.at[s])]

    def kv_pieces(core):
        cols = pl.ds(pl.multiple_of(core * 128, 128), 128)
        return [
            (kw.at[:, cols], lambda unit, s: unit.at[s, :, pl.ds(0, 128)]),
            (vw.at[:, cols], lambda unit, s: unit.at[s, :, pl.ds(128, 128)]),
        ]

    dpart.start_own(dn, down.at[me.chip, c])
    own_down = pltpu.make_async_copy(dn, down.at[me.chip, c], rsem.at[2])
    own_down.start()
    swap = pltpu.make_async_remote_copy(
        src_ref=residual, dst_ref=other, send_sem=rsem.at[0], recv_sem=rsem.at[1],
        device_id=me.dev(0, 0, 1 - c), device_id_type=MESH,
    )
    swap.start()
    qpart.start_pairs(q_pieces)
    kvpart.start_pairs(kv_pieces)

    def norm(source, first):
        def body(i, carry):
            rows = pl.ds(pl.multiple_of(i * 32, 32), 32)
            values = source[rows, :].astype(F32)
            factor = lax.rsqrt(jnp.mean(values * values, axis=1, keepdims=True) + EPS)
            target = pl.ds(pl.multiple_of(first + i * 32, 32), 32)
            normed[target, :] = (values * factor * gain[...].astype(F32)).astype(BF16)
            return carry

        lax.fori_loop(0, half // 32, body, 0)

    norm(residual, c * half)
    dpart.second_own()
    qpart.second_pairs()
    kvpart.second_pairs()
    swap.wait_recv()
    norm(other, (1 - c) * half)
    dpart.third()
    qpart.third()
    kvpart.third()
    dpart.fourth()
    for f in (0, 1, 3, 2):
        dpart.last(f)
    own_down.wait()

    first = me.chip * (2 * half)
    lanes = first + lax.broadcasted_iota(jnp.int32, (1, 2 * half), 1)
    unused, adapter = token_facts(lengths, lanes, adapters)
    part = dot(normed[...], down[...].reshape(D, 128), 1, 0).T
    kept = jnp.where(adapter == 2 * me.plane, part[0:48], 0.0) + jnp.where(
        adapter == 2 * me.plane + 1, part[48:96], 0.0
    )
    mixed[0] = kept[:, :half]
    mixed[1] = kept[:, half:]
    qpart.fourth()
    kvpart.fourth()
    trade = pltpu.make_async_remote_copy(
        src_ref=mixed.at[1 - c], dst_ref=mixed_in, send_sem=rsem.at[3], recv_sem=rsem.at[4],
        device_id=me.dev(0, 0, 1 - c), device_id_type=MESH,
    )
    trade.start()

    places = first + lax.broadcasted_iota(jnp.int32, (2 * half, HEAD), 0)
    start, unused = token_facts(lengths, places)
    angle = (places - start).astype(F32) * freq[...]
    cosine = jnp.cos(angle)
    sine = jnp.sin(angle)
    low = lax.broadcasted_iota(jnp.int32, (2 * half, HEAD), 1) < HEAD // 2
    sine = jnp.where(low, -sine, sine)

    trade.wait_recv()
    total = (mixed[c] + mixed_in[...]).astype(BF16)
    code_send[...] = total
    codes[me.plane, c] = total
    def chunk(buf, x):
        return buf[pl.ds(x * SIDE, SIDE)].reshape(D // SIDE, 256)

    def multiply(acc, buf, o, opening):
        x = lax.rem(me.x + o, SIDE)
        cols = pl.ds(pl.multiple_of(x * (D // SIDE), 128), D // SIDE)
        value = dot(normed[:, cols], chunk(buf, x), 1, 0)
        if opening:
            acc[...] = value
        else:
            acc[...] += value

    qpart.last(0)
    multiply(qacc, wq, 0, True)
    code_copies = []
    targets = [(0, 1 - c)] + [(dz, core) for dz in range(1, PLANES) for core in (c, 1 - c)]
    for n, (dz, core) in enumerate(targets):
        copy = pltpu.make_async_remote_copy(
            src_ref=code_send, dst_ref=codes.at[me.plane, c], send_sem=csend.at[n],
            recv_sem=crecv.at[me.plane, c], device_id=me.other_plane(dz, core), device_id_type=MESH,
        )
        copy.start()
        code_copies.append(copy)
    for f in (1, 3, 2):
        qpart.last(f)
        multiply(qacc, wq, f, False)
    for f in (0, 1, 3, 2):
        kvpart.last(f)
    for o in (0, 1, 3, 2):
        multiply(kvacc, wkv, o, o == 0)

    landed(codes.at[me.plane, 1 - c], crecv.at[me.plane, 1 - c])
    for dz in range(1, PLANES):
        z = lax.rem(me.plane + dz, PLANES)
        for core in (0, 1):
            landed(codes.at[z, core], crecv.at[z, core])
    whole = jnp.sum(codes[...].astype(F32), axis=0)
    whole = jnp.concatenate([whole[0], whole[1]], axis=1)

    def low_rank(slot, up, width):
        chosen = choose(whole[slot * RANK:(slot + 1) * RANK], adapter)
        cols = pl.ds(pl.multiple_of(c * width, width), width)
        return SCALE * dot(chosen, up[:, cols], 0, 0)

    def rotate(values):
        return values * cosine + pltpu.roll(values, HEAD // 2, 1) * sine

    query = qacc[...] + low_rank(0, upq, 256)
    q_out[:, :HEAD] = rotate(query[:, :HEAD]).astype(BF16)
    q_out[:, HEAD:] = rotate(query[:, HEAD:]).astype(BF16)
    k_out[...] = rotate(kvacc[:, :HEAD] + low_rank(1, upk, HEAD)).astype(BF16)
    v_out[...] = (kvacc[:, HEAD:] + low_rank(2, upv, HEAD)).astype(BF16)

    for copy in code_copies + [swap, trade]:
        copy.wait_send()
    for part in (dpart, qpart, kvpart):
        part.finish()


def attend_kernel(
    lengths, adapters, sinks, q, k, v, dn_out,
    att_out,
    kbuf, vbuf, top, total, acc,
    send, recv, own,
):
    me = Place()
    c = me.core
    tokens = q.shape[0]
    enter(plane_peers(me))
    kpart = Part(me, "xy", lambda j: kbuf.at[j], send.at[0], recv.at[0])
    vpart = Part(me, "yx", lambda j: vbuf.at[j], send.at[1], recv.at[1])
    kpart.start_own(k, kbuf.at[me.chip])
    vpart.start_own(v, vbuf.at[me.chip])

    first = me.chip * tokens
    places = first + lax.broadcasted_iota(jnp.int32, (1, tokens), 1)
    start, adapter = token_facts(lengths, places, adapters)
    for h in (0, 1):
        top[h] = jnp.full((1, tokens), sinks[2 * c + h], F32)
        total[h] = jnp.ones((1, tokens), F32)
        acc[h] = jnp.zeros((HEAD, tokens), F32)

    def block(key, value, chip):
        at = chip * tokens + lax.broadcasted_iota(jnp.int32, (tokens, tokens), 0)
        allowed = jnp.logical_and(at <= places, at >= start)
        for h in (0, 1):
            scores = dot(key, q[:, h * HEAD:(h + 1) * HEAD], 1, 1) * SCORE
            scores = jnp.where(allowed, scores, -1e30)
            old = top[h]
            fresh = jnp.maximum(old, jnp.max(scores, axis=0, keepdims=True))
            weights = jnp.exp(scores - fresh)
            factor = jnp.exp(old - fresh)
            total[h] = total[h] * factor + jnp.sum(weights, axis=0, keepdims=True)
            acc[h] = acc[h] * factor + dot(value, weights.astype(BF16), 0, 0)
            top[h] = fresh

    def visit(fx, fy):
        chip = me.chip_at(fx, fy)

        @pl.when(jnp.logical_and(chip < me.chip, chip + 8 >= me.chip))
        def _():
            block(kbuf[chip], vbuf[chip], chip)

    block(k[...], v[...], me.chip)
    kpart.second_own()
    vpart.second_own()
    kpart.third()
    vpart.third()
    kpart.fourth()
    vpart.fourth()

    def near(i, carry):
        a, b = i // 3, lax.rem(i, 3)
        visit(a + a // 2, b + b // 2)
        return carry

    lax.fori_loop(1, 9, near, 0)
    for f in (0, 1, 3, 2):
        kpart.last(f)
        vpart.last(f)

    def rest(i, carry):
        a = jnp.maximum(i - 4, 0)
        edge = i < 4
        visit(jnp.where(edge, 2, a + a // 2), jnp.where(edge, i, 2))
        return carry

    lax.fori_loop(0, 7, rest, 0)

    kpart.finish()
    vpart.finish()
    heads = jnp.concatenate([acc[0] / total[0], acc[1] / total[1]], axis=0).astype(BF16)
    att_out[0:2 * HEAD] = heads
    rows = pl.ds(pl.multiple_of(c * 256, 256), 256)
    terms = dot(dn_out[rows, :], heads, 0, 0)
    row = lax.broadcasted_iota(jnp.int32, terms.shape, 0) // RANK
    terms = jnp.where(row == adapter, terms, 0.0)
    terms = jnp.sum(terms.reshape(ADAPTERS, RANK, tokens), axis=0)
    att_out[2 * HEAD:2 * HEAD + RANK] = terms.astype(BF16)


def output_kernel(
    lengths, adapters, att, wo, up_out, post_gain, stream,
    out,
    ring, woa, wob, acc, swap_send, swap_in, square, squares,
    send, recv, zsend, zrecv, ssend, srecv, own,
):
    me = Place()
    c = me.core
    half = stream.shape[0]
    zpeers = [me.other_plane(dz) for dz in range(1, PLANES)]
    enter(plane_peers(me) + zpeers)

    subs = (pl.ds(0, 128), pl.ds(128, 144))
    zcopies = []

    def hop(src, slot, side, d, h):
        copy = pltpu.make_async_remote_copy(
            src_ref=src, dst_ref=ring.at[slot, subs[h]], send_sem=zsend.at[len(zcopies)],
            recv_sem=zrecv.at[side * 10 + d * 2 + h],
            device_id=me.other_plane(1 if side == 0 else PLANES - 1), device_id_type=MESH,
        )
        copy.start()
        zcopies.append(copy)

    def plane_of(side, d):
        return lax.rem(me.plane + (PLANES - d if side == 0 else d), PLANES)

    def arrive(side, d, h):
        landed(ring.at[plane_of(side, d), subs[h]], zrecv.at[side * 10 + d * 2 + h])

    for h in (0, 1):
        for side in (0, 1):
            hop(att.at[subs[h]], me.plane, side, 1, h)
    keep = pltpu.make_async_copy(att, ring.at[me.plane], own.at[0])
    keep.start()

    apart = Part(me, "xy", lambda j: woa.at[j], send.at[0], recv.at[0])
    bpart = Part(me, "yx", lambda j: wob.at[j], send.at[1], recv.at[1])

    def pieces(offset):
        def of(core):
            cols = pl.ds(pl.multiple_of(core * 256 + offset, 128), 128)
            return [(wo.at[:, cols], lambda unit, s: unit.at[s])]

        return of

    apart.start_pairs(pieces(0))
    bpart.start_pairs(pieces(128))

    def pass_on(d):
        for h in (0, 1):
            for side in (0, 1):
                arrive(side, d, h)
                if d < 3 or h == side:
                    slot = plane_of(side, d)
                    hop(ring.at[slot, subs[h]], slot, side, d + 1, h)

    def multiply(z, opening=False):
        weight = jnp.concatenate(
            [woa[pl.ds(2 * z, 2)].reshape(576, 128), wob[pl.ds(2 * z, 2)].reshape(576, 128)], axis=1
        )
        value = dot(weight, ring[z, pl.ds(0, 256)], 1, 0)
        if opening:
            acc[0:576] = value
        else:
            acc[0:576] += value

    apart.second_pairs()
    bpart.second_pairs()
    apart.third()
    bpart.third()
    pass_on(1)
    apart.fourth()
    bpart.fourth()
    pass_on(2)
    for f in (0, 1, 3, 2):
        apart.last(f)
        bpart.last(f)
    keep.wait()
    multiply(me.plane, True)
    for d in (1, 2):
        for side in (0, 1):
            multiply(plane_of(side, d))
    pass_on(3)
    for side in (0, 1):
        multiply(plane_of(side, 3))
    arrive(0, 4, 0)
    arrive(1, 4, 1)
    multiply(plane_of(0, 4))

    code_sum = jnp.sum(ring[:, pl.ds(256, RANK)].astype(F32), axis=0)
    theirs = pl.ds(pl.multiple_of((1 - c) * half, 256), half)
    mine = pl.ds(pl.multiple_of(c * half, 256), half)
    acc[576:592] = code_sum
    swap_send[...] = acc[:, theirs].astype(BF16)
    first = me.chip * (2 * half) + c * half
    places = first + lax.broadcasted_iota(jnp.int32, (1, half), 1)
    unused, adapter = token_facts(lengths, places, adapters)
    swap = pltpu.make_async_remote_copy(
        src_ref=swap_send, dst_ref=swap_in, send_sem=own.at[1], recv_sem=own.at[2],
        device_id=me.dev(0, 0, 1 - c), device_id_type=MESH,
    )
    swap.start()
    swap.wait_recv()
    merged = acc[:, mine] + swap_in[...].astype(F32)
    chosen = choose(merged[576:592].astype(BF16).astype(F32), adapter)
    projected = merged[0:576] + SCALE * dot(up_out[...], chosen, 0, 0)
    sums = jnp.sum(projected * projected, axis=0, keepdims=True)
    square[...] = jnp.broadcast_to(sums, square.shape)
    upright = projected.T
    scopies = []
    for dz in range(1, PLANES):
        copy = pltpu.make_async_remote_copy(
            src_ref=square, dst_ref=squares.at[me.plane], send_sem=ssend.at[dz],
            recv_sem=srecv.at[me.plane], device_id=me.other_plane(dz), device_id_type=MESH,
        )
        copy.start()
        scopies.append(copy)
    summed = square[...]
    for dz in range(1, PLANES):
        z = lax.rem(me.plane + dz, PLANES)
        landed(squares.at[z], srecv.at[z])
        summed = summed + squares[z]
    factor = lax.rsqrt(summed * (1.0 / D) + EPS).T[:, 0:1]
    out[...] = (
        stream[...].astype(F32) + upright * factor * post_gain[...].astype(F32)
    ).astype(BF16)
    for copy in zcopies + scopies + [swap]:
        copy.wait_send()
    apart.finish()
    bpart.finish()


VMEM = pl.BlockSpec(memory_space=pltpu.VMEM)
SMEM = pl.BlockSpec(memory_space=pltpu.SMEM)
ANY = pl.BlockSpec(memory_space=pl.ANY)
DMA = pltpu.SemaphoreType.DMA


def params(collective):
    return pltpu.CompilerParams(
        collective_id=collective, has_side_effects=True, vmem_limit_bytes=60 * 1024 * 1024
    )


def per_device(
    residual,
    pre_gain,
    query_weight,
    key_weight,
    value_weight,
    output_weight,
    adapter_down,
    adapter_up_query,
    adapter_up_key,
    adapter_up_value,
    adapter_down_out,
    adapter_up_out,
    post_gain,
    sink_logits,
    prompt_lengths,
    prompt_adapters,
):
    half = residual.shape[0]
    tokens = 2 * half
    own_width = adapter_up_out.shape[1]
    exponent = np.arange(HEAD // 2, dtype=np.float32) * np.float32(2.0 / HEAD)
    freq = np.power(np.float32(10000.0), -exponent).astype(np.float32)
    freq = jnp.asarray(np.concatenate([freq, freq])[None, :])

    exchange = []
    for z in range(PLANES):
        for w in range(2 * CHIPS):
            exchange.append((w * PLANES + z, (4 * z + w % 4) * PLANES + w // 4))
    turned = lax.ppermute(output_weight.T, ("wide", "narrow"), exchange)
    down = jnp.pad(adapter_down, ((0, 0), (0, HEAD - adapter_down.shape[1])))
    stream = lax.dynamic_slice_in_dim(residual, lax.axis_index("narrow") * own_width, own_width, 1)

    shape = jax.ShapeDtypeStruct
    q, k, v = pl.pallas_call(
        project_kernel,
        name="project",
        out_shape=(
            shape((tokens, 2 * HEAD), BF16),
            shape((tokens, HEAD), BF16),
            shape((tokens, HEAD), BF16),
        ),
        in_specs=[SMEM, SMEM, VMEM, VMEM, ANY, ANY, ANY, ANY, VMEM, VMEM, VMEM, VMEM],
        out_specs=(VMEM, VMEM, VMEM),
        scratch_shapes=[
            pltpu.VMEM((half, D), BF16),
            pltpu.VMEM((tokens, D), BF16),
            pltpu.VMEM((CHIPS, 2, ROWS, 256), BF16),
            pltpu.VMEM((CHIPS, 2, ROWS, 256), BF16),
            pltpu.VMEM((CHIPS, 2, ROWS, 128), BF16),
            pltpu.VMEM((tokens, 256), F32),
            pltpu.VMEM((tokens, 256), F32),
            pltpu.VMEM((2, 48, half), F32),
            pltpu.VMEM((48, half), F32),
            pltpu.VMEM((48, half), BF16),
            pltpu.VMEM((PLANES, 2, 48, half), BF16),
            DMA((3, 32)),
            DMA((3, 24)),
            DMA((15,)),
            DMA((PLANES, 2)),
            DMA((5,)),
        ],
        compiler_params=params(0),
    )(
        prompt_lengths, prompt_adapters, residual, pre_gain[None, :], query_weight, key_weight,
        value_weight, down, adapter_up_query, adapter_up_key, adapter_up_value, freq,
    )
    att = pl.pallas_call(
        attend_kernel,
        name="attend",
        out_shape=shape((2 * HEAD + RANK, tokens), BF16),
        in_specs=[SMEM, SMEM, SMEM, VMEM, VMEM, VMEM, VMEM],
        out_specs=VMEM,
        scratch_shapes=[
            pltpu.VMEM((CHIPS, tokens, HEAD), BF16),
            pltpu.VMEM((CHIPS, tokens, HEAD), BF16),
            pltpu.VMEM((2, 1, tokens), F32),
            pltpu.VMEM((2, 1, tokens), F32),
            pltpu.VMEM((2, HEAD, tokens), F32),
            DMA((2, 32)),
            DMA((2, 24)),
            DMA((1,)),
        ],
        compiler_params=params(1),
    )(prompt_lengths, prompt_adapters, sink_logits, q, k, v, adapter_down_out)
    return pl.pallas_call(
        output_kernel,
        name="output",
        out_shape=shape((half, own_width), BF16),
        in_specs=[SMEM, SMEM, VMEM, ANY, VMEM, VMEM, VMEM],
        out_specs=VMEM,
        scratch_shapes=[
            pltpu.VMEM((PLANES, 2 * HEAD + RANK, tokens), BF16),
            pltpu.VMEM((CHIPS, 2, ROWS, HEAD), BF16),
            pltpu.VMEM((CHIPS, 2, ROWS, HEAD), BF16),
            pltpu.VMEM((own_width + RANK, tokens), F32),
            pltpu.VMEM((own_width + RANK, half), BF16),
            pltpu.VMEM((own_width + RANK, half), BF16),
            pltpu.VMEM((8, half), F32),
            pltpu.VMEM((PLANES, 8, half), F32),
            DMA((2, 32)),
            DMA((2, 24)),
            DMA((16,)),
            DMA((20,)),
            DMA((8,)),
            DMA((8,)),
            DMA((3,)),
        ],
        compiler_params=params(2),
    )(
        prompt_lengths, prompt_adapters, att, turned, adapter_up_out, post_gain[None, :], stream
    )


def solution(mesh):
    return jax.shard_map(
        per_device,
        mesh=mesh,
        in_specs=(
            P("wide", None),
            P(),
            P("wide", "narrow"),
            P("wide", "narrow"),
            P("wide", "narrow"),
            P("narrow", "wide"),
            P("wide", "narrow"),
            P(None, "narrow"),
            P(None, "narrow"),
            P(None, "narrow"),
            P("narrow", None),
            P(None, "narrow"),
            P("narrow"),
            P("narrow"),
            P(),
            P(),
        ),
        out_specs=P("wide", "narrow"),
        check_vma=False,
    )
```

time: 510 us -> 156 us (0.31)
  waiting for transfers between devices: 337 us -> 0.01 us
  Pallas kernels: 0 us -> 144 us
  matrix products: 54.8 us -> 0 us
  blocking collectives: 50.4 us -> 0 us
  other arithmetic: 40 us -> 0 us
  between operations: 13.8 us -> 0.03 us
    all_gather x6 -> x0, waiting for transfers between devices: 190 us -> none  [the longest x1 46.4 us: per_device(): piece_keys = lax.all_gather(keys, 'wide', axis=0, tiled=True)]
    psum x2 -> x0, waiting for transfers between devices: 145 us -> none  [the longest x1 81.8 us: per_device(): lax.psum(partial_out.astype(jnp.bfloat16), 'narrow').astype(jnp.float32)]
    pallas_call x0 -> x3, Pallas kernels: none -> 144 us  [the longest x1 58.8 us: per_device(): pl.pallas_call(project_kernel, name='project', out_shape=(shape((tokens,...]
    dot_general x12 -> x0, matrix products: 54.8 us -> none  [the longest x1 16.1 us: per_device(): jnp.einsum('qgjd,kgd->qgjk', queries, piece_keys, preferred_element_type=...]
    all_gather x2 -> x0, blocking collectives: 50.4 us -> none  [the longest x1 27.4 us: per_device(): lax.all_gather(adapter_down, 'wide', axis=0, tiled=True)]
    reduce_sum x5 -> x0, other arithmetic: 20.5 us -> none  [the longest x1 15 us: per_device(): total = total * factor + jnp.sum(weights, axis=-1)]
    convert_element_type x8 -> x0, other arithmetic: 11.2 us -> none  [the longest x1 4 us: per_device(): partial_out.astype(jnp.bfloat16)]
  transfers between devices with their start and end apart: 8 -> 1, of which waited for: 7 -> 0; matrix products, arithmetic and copies ran while one was open for 17% -> 5% of each run, Pallas kernels for 0% -> 59%
where the time goes in v1:
time: 156 us
  Pallas kernels  144 us (92%)
  local copies, waits for them, and re-layouts  10.2 us (7%)
  starting transfers between devices  1.56 us (1%)
    pallas_call x1, Pallas kernels, per_device(): pl.pallas_call(project_kernel, name='project', out_shape=(shape((tokens,...  58.8 us
    pallas_call x1, Pallas kernels, per_device(): pl.pallas_call(output_kernel, name='output', out_shape=shape((half, own_w...  52.1 us
    pallas_call x1, Pallas kernels, per_device(): pl.pallas_call(attend_kernel, name='attend', out_shape=shape((2 * HEAD +...  32.9 us
  transfers between devices with their start and end apart: 1, of which 0 were waited for; matrix products, arithmetic and copies ran while one was open for 5% of the time, Pallas kernels for 59%

profile of v1, /device:TPU:1, one launch (start us, length us, event | category | flops | bytes accessed | tf_op | source)
XLA Modules:
  0.0 155.6 jit_solution(14548149248329072476)
XLA Ops:
  0.0 1.6 %collective-permute-start = (bf16[144,512]{1,0:T(8,128)(2,1)}, bf16[144,512]{1,0:T(8,128)(2,1)S(1)}, u32[]{:S(2)}, u32[]{:S(2)}) collective-permute-start(bf16[144,512]{1,0:T(8,128)(2,1)} %bitcast.1), channel_id=1, source_target_pairs={{0,0},{8,8},{16,16},{24,24},{32,1},{40,9},{48,17},{56,25},{64,2},{... | collective-permute-start | bytes 442376 | tf_op jit(solution)/shard_map/ppermute | solution.py:600
  1.6 1.3 broadcast_in_dim.6.gain
  2.9 1.9 %copy.18.up_out = bf16[256,576]{1,0:T(8,128)(2,1)} copy(bf16[256,576]{0,1:T(8,128)(2,1)} %param.28) | data formatting | bytes 589824 | tf_op args[11]
  4.7 1.3 broadcast_in_dim.7.post_gain
  6.0 1.4 pad.4.dn
  7.4 58.8 %project.1 = (bf16[512,256]{1,0:T(8,128)(2,1)}, bf16[512,128]{1,0:T(8,128)(2,1)}, bf16[512,128]{1,0:T(8,128)(2,1)}) custom-call(s32[4]{0:T(128)} %lengths.5, s32[4]{0:T(128)} %adapters.5, bf16[256,4608]{1,0:T(8,128)(2,1)} %residual.1, bf16[1,4608]{1,0:T(2,128)(2,1)} %broadcast_in_dim.6.gain, bf16[144,512]{1,0:T(8,128)(2,1)} %qw.1, bf16[144,256]{1,0:T(8,128)(2,1)} %kw.1, ...), custom_call_target="tpu_custom_call" | custom-call | tf_op jit(solution)/shard_map/project/pallas_call | solution.py:605
  66.2 32.9 %attend.1.att = bf16[272,512]{1,0:T(8,128)(2,1)} custom-call(s32[4]{0:T(128)} %lengths.5, s32[4]{0:T(128)} %adapters.5, f32[4]{0:T(128)} %sinks.1, bf16[512,256]{1,0:T(8,128)(2,1)} %get-tuple-element.8.q, bf16[512,128]{1,0:T(8,128)(2,1)} %get-tuple-element.9.k, bf16[512,128]{1,0:T(8,128)(2,1)} %get-tuple-element.10.v, bf16[512,256]{1,0:T(8,128)(2,1)} %dn_out.1), custom_call_target="tpu_custom_call" | custom-call | tf_op jit(solution)/shard_map/attend/pallas_call | solution.py:638
  99.1 1.9 %constant_dynamic-slice_fusion.stream = bf16[256,576]{1,0:T(8,128)(2,1)} fusion(bf16[256,4608]{1,0:T(8,128)(2,1)} %residual.1, s32[]{:T(128)S(6)} %select_n.3), kind=kLoop, calls=%fused_computation | loop fusion | bytes 589828 | tf_op jit(solution)/shard_map/dynamic_slice | solution.py:602
  101.0 0.0 collective-permute-done.wo
  101.0 0.0 copy-start
  101.0 0.7 copy-done
  101.6 52.1 %output.1 = bf16[256,576]{1,0:T(8,128)(2,1)} custom-call(s32[4]{0:T(128)} %lengths.5, s32[4]{0:T(128)} %adapters.5, bf16[272,512]{1,0:T(8,128)(2,1)} %attend.1.att, bf16[144,512]{1,0:T(8,128)(2,1)} %copy-done, bf16[256,576]{1,0:T(8,128)(2,1)} %copy.18.up_out, bf16[1,576]{1,0:T(2,128)(2,1)} %broadcast_in_dim.7.post_gain, ...), custom_call_target="tpu_custom_call" | custom-call | tf_op jit(solution)/shard_map/output/pallas_call | solution.py:656
  153.7 1.8 %copy.19 = bf16[256,576]{0,1:T(8,128)(2,1)} copy(bf16[256,576]{1,0:T(8,128)(2,1)} %output.1) | data formatting | bytes 589824 | tf_op jit(solution)/shard_map/output/pallas_call | solution.py:656
Async XLA Ops:
  0.0 101.0 %collective-permute-start = (bf16[144,512]{1,0:T(8,128)(2,1)}, bf16[144,512]{1,0:T(8,128)(2,1)S(1)}, u32[]{:S(2)}, u32[]{:S(2)}) collective-permute-start(bf16[144,512]{1,0:T(8,128)(2,1)} %bitcast.1), channel_id=1, source_target_pairs={{0,0},{8,8},{16,16},{24,24},{32,1},{40,9},{48,17},{56,25},{64,2},{... | collective-permute-start | bytes 442376 | tf_op jit(solution)/shard_map/ppermute | solution.py:600
  101.0 0.7 copy-start

commit v2 on v1

v2 whole, which is shorter than its diff:
```python
import functools

import jax
import jax.numpy as jnp
import numpy as np
from jax import lax
from jax.experimental import pallas as pl
from jax.experimental.pallas import tpu as pltpu
from jax.sharding import PartitionSpec as P

MESH = pl.DeviceIdType.MESH
HEAD = 128
ADAPTERS = 16
RANK = 16
D = 4608
SIDE = 4
CHIPS = 16
PLANES = 8
ROWS = D // (2 * CHIPS)
EPS = 1e-06
SCALE = 0.5
SCORE = 1.0 / 12.0
F32 = jnp.float32
BF16 = jnp.bfloat16


def dot(a, b, ca, cb):
    return lax.dot_general(a, b, (((ca,), (cb,)), ((), ())), preferred_element_type=F32)


class Place:
    def __init__(self):
        wide = lax.axis_index("wide")
        self.plane = lax.axis_index("narrow")
        self.core = lax.rem(wide, 2)
        self.chip = wide // 2
        self.x = self.chip // SIDE
        self.y = lax.rem(self.chip, SIDE)
        self.wide = wide

    def chip_at(self, dx, dy):
        return lax.rem(self.x + dx, SIDE) * SIDE + lax.rem(self.y + dy, SIDE)

    def dev(self, dx, dy, core):
        return (self.chip_at(dx, dy) * 2 + core, self.plane)

    def other_plane(self, dz, core=None):
        core = self.core if core is None else core
        return (self.chip * 2 + core, lax.rem(self.plane + dz, PLANES))


def plane_peers(me):
    peers = [me.dev(0, 0, 1 - me.core)]
    for dx, dy in ((1, 0), (3, 0), (0, 1), (0, 3)):
        peers += [me.dev(dx, dy, 0), me.dev(dx, dy, 1)]
    return peers


def landed(ref, sem):
    pltpu.make_async_copy(ref, ref, sem).wait()


class Part:
    def __init__(self, me, order, unit, send, recv):
        self.me, self.order, self.unit, self.send, self.recv = me, order, unit, send, recv
        self.sent = []

    def rel(self, f, g):
        return (f, g) if self.order == "xy" else (g, f)

    def at(self, f, g):
        return self.unit(self.me.chip_at(*self.rel(f, g)))

    def target(self, f, g, core):
        return self.me.dev(*self.rel(f, g), core)

    def push(self, src, dst, sem, device):
        copy = pltpu.make_async_remote_copy(
            src_ref=src,
            dst_ref=dst,
            send_sem=self.send.at[len(self.sent)],
            recv_sem=sem,
            device_id=device,
            device_id_type=MESH,
        )
        copy.start()
        self.sent.append(copy)

    def label(self, f, g):
        return self.recv.at[f * 4 + g]

    def single(self, f, s):
        return self.recv.at[16 + f * 2 + s]

    def start_pairs(self, pieces):
        me = self.me
        mine = self.unit(me.chip)
        for d in (1, 3):
            for core in (me.core, 1 - me.core):
                for src, sub in pieces(core):
                    self.push(src, sub(mine, me.core), self.single(4 - d, me.core), self.target(d, 0, core))
        for src, sub in pieces(1 - me.core):
            self.push(src, sub(mine, me.core), self.single(0, me.core), self.target(0, 0, 1 - me.core))
        for n, (src, sub) in enumerate(pieces(me.core)):
            pltpu.make_async_copy(src, sub(mine, me.core), self.single(0, me.core)).start()

    def start_own(self, src, dst):
        self.own = src
        for d in (1, 3):
            self.push(src, dst, self.label(4 - d, 0), self.target(d, 0, self.me.core))

    def far(self):
        return 3 - 2 * self.me.core, 1 + 2 * self.me.core

    def spread(self, f, src=None):
        unit = self.at(f, 0)
        for d in (1, 3):
            self.push(unit if src is None else src, unit, self.label(f, 4 - d), self.target(0, d, self.me.core))

    def second_pairs(self):
        landed(self.at(0, 0).at[0], self.single(0, 0))
        landed(self.at(0, 0).at[1], self.single(0, 1))
        self.spread(0)
        for f in (1, 3):
            for s in (0, 1):
                landed(self.at(f, 0).at[s], self.single(f, s))
        self.after_first()

    def second_own(self):
        self.spread(0, self.own)
        self.second_rest()

    def second_rest(self):
        for f in (1, 3):
            landed(self.at(f, 0), self.label(f, 0))
        self.after_first()

    def after_first(self):
        source, step = self.far()
        unit = self.at(source, 0)
        self.push(unit, unit, self.label(2, 0), self.target(step, 0, self.me.core))
        for f in (1, 3):
            self.spread(f)

    def third(self):
        landed(self.at(2, 0), self.label(2, 0))
        self.spread(2)

    def fourth(self, fs=(0, 1, 3, 2)):
        source, step = self.far()
        for f in fs:
            for g in (1, 3):
                landed(self.at(f, g), self.label(f, g))
            unit = self.at(f, source)
            self.push(unit, unit, self.label(f, 2), self.target(0, step, self.me.core))

    def last(self, f):
        landed(self.at(f, 2), self.label(f, 2))

    def finish(self):
        for copy in self.sent:
            copy.wait_send()


def token_facts(lengths, places, adapters=None):
    start = jnp.zeros_like(places)
    adapter = jnp.zeros_like(places)
    begin = jnp.int32(0)
    for p in range(4):
        end = begin + lengths[p]
        member = jnp.logical_and(places >= begin, places < end)
        start = jnp.where(member, begin, start)
        if adapters is not None:
            adapter = jnp.where(member, adapters[p], adapter)
        begin = end
    return start, adapter


def choose(codes, adapter):
    tokens = codes.shape[1]
    spread = jnp.broadcast_to(codes[None], (ADAPTERS, RANK, tokens)).reshape(ADAPTERS * RANK, tokens)
    row = lax.broadcasted_iota(jnp.int32, (ADAPTERS * RANK, tokens), 0) // RANK
    return jnp.where(row == adapter, spread, 0.0).astype(BF16)


def layer_kernel(
    lengths, adapters, sinks, residual, gain, qw, kw, vw, dn, wo, upq, upk, upv, dn_out, up_out, post_gain, freq,
    out,
    raw, normed, wk, wv, wq0, wq1, down, acc, mixed, mixed_in, code_send, codes, code_half,
    query, key, value, kbuf, vbuf, top, total, head_acc, att,
    ring, wo_in, woa, wob, out_acc, swap_send, swap_in, square, squares, stream,
    send, recv, csend, crecv, zsend, zrecv, ssend, srecv, one,
):
    me = Place()
    c = me.core
    half = residual.shape[0]
    tokens = 2 * half
    partner = me.dev(0, 0, 1 - c)
    trade_wide = 4 * me.plane + lax.rem(me.wide, 4)
    trade_plane = me.wide // 4
    foreign = trade_plane != me.plane

    own_rows = pltpu.make_async_copy(residual, raw.at[c], one.at[0])
    own_rows.start()
    own_down = pltpu.make_async_copy(dn, down.at[me.chip, c], one.at[1])
    barrier = pltpu.get_barrier_semaphore()
    peers = plane_peers(me) + [me.other_plane(dz) for dz in range(1, PLANES)]
    for peer in peers:
        pl.semaphore_signal(barrier, inc=1, device_id=peer, device_id_type=MESH)

    @pl.when(foreign)
    def _():
        pl.semaphore_signal(barrier, inc=1, device_id=(trade_wide, trade_plane), device_id_type=MESH)

    for j in range(CHIPS):
        down[j, 1 - c] = jnp.zeros(down.shape[2:], BF16)
    pl.semaphore_wait(barrier, len(peers) + foreign.astype(jnp.int32))

    def part(n, order, buf):
        return Part(me, order, lambda j: buf.at[j], send.at[n], recv.at[n])

    dpart = Part(me, "xy", lambda j: down.at[j, c], send.at[0], recv.at[0])
    kpart, vpart = part(1, "xy", wk), part(2, "yx", wv)
    q0part, q1part = part(3, "xy", wq0), part(4, "yx", wq1)
    keys, values = part(5, "xy", kbuf), part(6, "yx", vbuf)
    apart, bpart = part(7, "xy", woa), part(8, "yx", wob)

    def pieces(source, width, offset):
        def of(core):
            cols = pl.ds(pl.multiple_of(core * width + offset, HEAD), HEAD)
            return [(source.at[:, cols], lambda unit, s: unit.at[s])]

        return of

    def local(src, dst, sem):
        copy = pltpu.make_async_copy(src, dst, sem)
        copy.start()
        return copy

    def remote(src, dst, sems, device):
        copy = pltpu.make_async_remote_copy(
            src_ref=src, dst_ref=dst, send_sem=sems[0], recv_sem=sems[1],
            device_id=device, device_id_type=MESH,
        )
        copy.start()
        return copy

    dpart.start_own(dn, down.at[me.chip, c])
    own_down.start()
    swap_rows = remote(residual, raw.at[c], (one.at[2], one.at[3]), partner)
    kpart.start_pairs(pieces(kw, HEAD, 0))
    vpart.start_pairs(pieces(vw, HEAD, 0))
    q0part.start_pairs(pieces(qw, 2 * HEAD, 0))
    q1part.start_pairs(pieces(qw, 2 * HEAD, HEAD))

    gain_row = gain[...].astype(F32).reshape(1, D)

    def norm(side, begin, end):
        def body(i, carry):
            rows = pl.ds(pl.multiple_of(i * 32, 32), 32)
            source = raw[side, rows, :].astype(F32)
            factor = lax.rsqrt(jnp.mean(source * source, axis=1, keepdims=True) + EPS)
            target = pl.ds(pl.multiple_of(side * half + i * 32, 32), 32)
            normed[target, :] = (source * factor * gain_row).astype(BF16)
            return carry

        lax.fori_loop(begin, end, body, 0)

    own_rows.wait()
    norm(c, 0, half // 32)
    dpart.second_own()
    kpart.second_pairs()
    vpart.second_pairs()
    for p in (dpart, kpart, vpart):
        p.third()
    for p in (dpart, kpart, vpart):
        p.fourth((0, 1, 3))
    q0part.second_pairs()
    q1part.second_pairs()
    for p in (dpart, kpart, vpart):
        p.fourth((2,))
    swap_rows.wait_recv()
    norm(1 - c, 0, half // 64)
    q0part.third()
    q1part.third()
    norm(1 - c, half // 64, half // 32)

    first = me.chip * tokens
    places = first + lax.broadcasted_iota(jnp.int32, (1, tokens), 1)
    start_row, adapter = token_facts(lengths, places, adapters)
    for f in (0, 1, 3, 2):
        dpart.last(f)
    own_down.wait()
    part_codes = dot(normed[...], down[...].reshape(D, 96), 1, 0).T
    kept = jnp.where(adapter == 2 * me.plane, part_codes[0:48], 0.0) + jnp.where(
        adapter == 2 * me.plane + 1, part_codes[48:96], 0.0
    )
    mixed[0] = kept[:, :half]
    mixed[1] = kept[:, half:]
    for p in (q0part, q1part):
        p.fourth((0, 1, 3))
    trade = remote(mixed.at[1 - c], mixed_in, (one.at[4], one.at[5]), partner)

    token = first + lax.broadcasted_iota(jnp.int32, (tokens, HEAD), 0)
    start, unused = token_facts(lengths, token)
    angle = (token - start).astype(F32) * freq[...]
    cosine = jnp.cos(angle)
    sine = jnp.sin(angle)
    sine = jnp.where(lax.broadcasted_iota(jnp.int32, (tokens, HEAD), 1) < HEAD // 2, -sine, sine)

    trade.wait_recv()
    code_send[...] = (mixed[c] + mixed_in[...]).astype(BF16)
    for p in (q0part, q1part):
        p.fourth((2,))
    code_copies = []
    for dz in (4, 3, 5, 2, 6, 1, 7):
        code_copies.append(
            remote(code_send, codes.at[me.plane], (csend.at[dz], crecv.at[me.plane]), me.other_plane(dz))
        )
    wo_copy = pltpu.make_async_remote_copy(
        src_ref=wo, dst_ref=wo_in, send_sem=one.at[6], recv_sem=one.at[7],
        device_id=(trade_wide, trade_plane), device_id_type=MESH,
    )

    @pl.when(foreign)
    def _():
        wo_copy.start()

    @pl.when(jnp.logical_not(foreign))
    def _():
        pltpu.make_async_copy(wo, wo_in, one.at[7]).start()

    def multiply(left, right, o):
        x = lax.rem(me.x + o, SIDE)
        cols = pl.ds(pl.multiple_of(x * (D // SIDE), 128), D // SIDE)
        rows = pl.ds(x * SIDE, SIDE)
        weight = jnp.concatenate(
            [left[rows].reshape(D // SIDE, HEAD), right[rows].reshape(D // SIDE, HEAD)], axis=1
        )
        result = dot(normed[:, cols], weight, 1, 0)
        if o == 0:
            acc[...] = result
        else:
            acc[...] += result

    for f in (0, 1, 3, 2):
        kpart.last(f)
        vpart.last(f)
    for o in (0, 1, 3, 2):
        multiply(wk, wv, o)

    whole = code_send[...].astype(F32)
    for dz in (1, 7, 2, 6, 3, 5, 4):
        z = lax.rem(me.plane + dz, PLANES)
        landed(codes.at[z], crecv.at[z])
        whole = whole + codes[z].astype(F32)
    code_half[c] = whole.astype(BF16)
    trade_codes = remote(code_half.at[c], code_half.at[c], (one.at[8], one.at[9]), partner)
    trade_codes.wait_recv()
    whole = jnp.concatenate([code_half[0], code_half[1]], axis=1).astype(F32)

    def low_rank(slot, up, width):
        chosen = choose(whole[slot * RANK:(slot + 1) * RANK], adapter)
        cols = pl.ds(pl.multiple_of(c * width, width), width)
        return SCALE * dot(chosen, up[:, cols], 0, 0)

    def rotate(x):
        return x * cosine + pltpu.roll(x, HEAD // 2, 1) * sine

    key[...] = rotate(acc[:, :HEAD] + low_rank(1, upk, HEAD)).astype(BF16)
    value[...] = (acc[:, HEAD:] + low_rank(2, upv, HEAD)).astype(BF16)
    for h in (0, 1):
        top[h] = jnp.full((1, tokens), sinks[2 * c + h], F32)
        total[h] = jnp.ones((1, tokens), F32)
        head_acc[h] = jnp.zeros((HEAD, tokens), F32)
    keys.start_own(key, kbuf.at[me.chip])
    values.start_own(value, vbuf.at[me.chip])
    keys.spread(0, key)
    values.spread(0, value)

    for f in (0, 1, 3, 2):
        q0part.last(f)
        q1part.last(f)
    for o in (0, 1, 3, 2):
        multiply(wq0, wq1, o)
    full = acc[...] + low_rank(0, upq, 2 * HEAD)
    query[:, :HEAD] = rotate(full[:, :HEAD]).astype(BF16)
    query[:, HEAD:] = rotate(full[:, HEAD:]).astype(BF16)
    keys.second_rest()
    values.second_rest()

    def block(k, v, chip, heads):
        at = chip * tokens + lax.broadcasted_iota(jnp.int32, (tokens, tokens), 0)
        allowed = jnp.logical_and(at <= places, at >= start_row)
        for h in heads:
            scores = dot(k, query[:, h * HEAD:(h + 1) * HEAD], 1, 1) * SCORE
            scores = jnp.where(allowed, scores, -1e30)
            old = top[h]
            fresh = jnp.maximum(old, jnp.max(scores, axis=0, keepdims=True))
            weights = jnp.exp(scores - fresh)
            factor = jnp.exp(old - fresh)
            total[h] = total[h] * factor + jnp.sum(weights, axis=0, keepdims=True)
            head_acc[h] = head_acc[h] * factor + dot(v, weights.astype(BF16), 0, 0)
            top[h] = fresh

    def visit(fx, fy, heads):
        chip = me.chip_at(fx, fy)

        @pl.when(jnp.logical_and(chip < me.chip, chip + 8 >= me.chip))
        def _():
            block(kbuf[chip], vbuf[chip], chip, heads)

    block(key[...], value[...], me.chip, (0, 1))
    keys.third()
    values.third()
    keys.fourth()
    values.fourth()
    landed(wo_in, one.at[7])
    apart.start_pairs(pieces(wo_in, 2 * HEAD, 0))
    bpart.start_pairs(pieces(wo_in, 2 * HEAD, HEAD))

    def near(i, carry):
        a, b = i // 3, lax.rem(i, 3)
        visit(a + a // 2, b + b // 2, (0, 1))
        return carry

    lax.fori_loop(1, 9, near, 0)
    for f in (0, 1, 3, 2):
        keys.last(f)
        values.last(f)
    apart.second_pairs()
    bpart.second_pairs()

    subs = (pl.ds(0, 128), pl.ds(128, 144))
    zcopies = []

    def hop(src, slot, side, d, h):
        zcopies.append(
            remote(
                src, ring.at[slot, subs[h]], (zsend.at[len(zcopies)], zrecv.at[side * 10 + d * 2 + h]),
                me.other_plane(1 if side == 0 else PLANES - 1),
            )
        )

    def plane_of(side, d):
        return lax.rem(me.plane + (PLANES - d if side == 0 else d), PLANES)

    def arrive(side, d, h):
        landed(ring.at[plane_of(side, d), subs[h]], zrecv.at[side * 10 + d * 2 + h])

    dn_cols = pl.multiple_of(c * 256, 256)
    row = lax.broadcasted_iota(jnp.int32, (ADAPTERS * RANK, tokens), 0) // RANK
    for h in (0, 1):
        def rest(i, carry):
            a = jnp.maximum(i - 4, 0)
            edge = i < 4
            visit(jnp.where(edge, 2, a + a // 2), jnp.where(edge, i, 2), (h,))
            return carry

        lax.fori_loop(0, 7, rest, 0)
        att[h * HEAD:(h + 1) * HEAD] = (head_acc[h] / total[h]).astype(BF16)
        if h == 1:
            terms = dot(dn_out[pl.ds(dn_cols, 2 * HEAD), :], att[0:2 * HEAD], 0, 0)
            terms = jnp.where(row == adapter, terms, 0.0)
            terms = jnp.sum(terms.reshape(ADAPTERS, RANK, tokens), axis=0)
            att[2 * HEAD:2 * HEAD + RANK] = terms.astype(BF16)
        for side in (0, 1):
            hop(att.at[subs[h]], me.plane, side, 1, h)
    keep = local(att, ring.at[me.plane], one.at[10])

    def pass_on(d):
        for h in (0, 1):
            for side in (0, 1):
                arrive(side, d, h)
                if d < 3 or h == side:
                    slot = plane_of(side, d)
                    hop(ring.at[slot, subs[h]], slot, side, d + 1, h)

    def out_multiply(z, opening=False):
        weight = jnp.concatenate(
            [woa[pl.ds(2 * z, 2)].reshape(576, 128), wob[pl.ds(2 * z, 2)].reshape(576, 128)], axis=1
        )
        result = dot(weight, ring[z, pl.ds(0, 256)], 1, 0)
        if opening:
            out_acc[0:576] = result
        else:
            out_acc[0:576] += result

    apart.third()
    bpart.third()
    pass_on(1)
    apart.fourth()
    bpart.fourth()
    odd = lax.rem(me.plane, 2) * 64
    window = pl.ds(pl.multiple_of(me.plane * 576 - odd, 128), 640)
    stream[...] = raw[c, :, window].astype(F32).T
    post = jnp.broadcast_to(post_gain[...].astype(F32).reshape(1, 576), (half, 576)).T
    pass_on(2)
    for f in (0, 1, 3, 2):
        apart.last(f)
        bpart.last(f)
    keep.wait()
    out_multiply(me.plane, True)
    for d in (1, 2):
        for side in (0, 1):
            out_multiply(plane_of(side, d))
    pass_on(3)
    for side in (0, 1):
        out_multiply(plane_of(side, 3))
    arrive(0, 4, 0)
    arrive(1, 4, 1)
    out_multiply(plane_of(0, 4))

    out_acc[576:592] = jnp.sum(ring[:, pl.ds(256, RANK)].astype(F32), axis=0)
    theirs = pl.ds(pl.multiple_of((1 - c) * half, 256), half)
    mine = pl.ds(pl.multiple_of(c * half, 256), half)
    swap_send[...] = out_acc[:, theirs].astype(BF16)
    own_places = first + c * half + lax.broadcasted_iota(jnp.int32, (1, half), 1)
    unused, own_adapter = token_facts(lengths, own_places, adapters)
    swap = remote(swap_send, swap_in, (one.at[11], one.at[12]), partner)
    swap.wait_recv()
    merged = out_acc[:, mine] + swap_in[...].astype(F32)
    chosen = choose(merged[576:592].astype(BF16).astype(F32), own_adapter)
    projected = merged[0:576] + SCALE * dot(up_out[...], chosen, 1, 0)
    sums = jnp.sum(projected * projected, axis=0, keepdims=True)
    square[...] = jnp.broadcast_to(sums, square.shape)
    scopies = []
    for dz in (4, 3, 5, 2, 6, 1, 7):
        scopies.append(
            remote(square, squares.at[me.plane], (ssend.at[dz], srecv.at[me.plane]), me.other_plane(dz))
        )
    weighted = projected * post
    summed = square[...]
    for dz in range(1, PLANES):
        z = lax.rem(me.plane + dz, PLANES)
        landed(squares.at[z], srecv.at[z])
        summed = summed + squares[z]
    factor = lax.rsqrt(summed[0:1] * (1.0 / D) + EPS)
    out[...] = (stream[pl.ds(pl.multiple_of(odd, 64), 576), :] + weighted * factor).astype(BF16)

    for copy in code_copies + zcopies + scopies + [swap_rows, trade, trade_codes, swap]:
        copy.wait_send()
    for p in (dpart, kpart, vpart, q0part, q1part, keys, values, apart, bpart):
        p.finish()

    @pl.when(foreign)
    def _():
        wo_copy.wait_send()


VMEM = pl.BlockSpec(memory_space=pltpu.VMEM)
SMEM = pl.BlockSpec(memory_space=pltpu.SMEM)
ANY = pl.BlockSpec(memory_space=pl.ANY)
DMA = pltpu.SemaphoreType.DMA


def per_device(
    residual,
    pre_gain,
    query_weight,
    key_weight,
    value_weight,
    output_weight,
    adapter_down,
    adapter_up_query,
    adapter_up_key,
    adapter_up_value,
    adapter_down_out,
    adapter_up_out,
    post_gain,
    sink_logits,
    prompt_lengths,
    prompt_adapters,
):
    half = residual.shape[0]
    tokens = 2 * half
    own_width = adapter_up_out.shape[1]
    exponent = np.arange(HEAD // 2, dtype=np.float32) * np.float32(2.0 / HEAD)
    freq = np.power(np.float32(10000.0), -exponent).astype(np.float32)
    freq = jnp.asarray(np.concatenate([freq, freq])[None, :])
    piece = pltpu.VMEM((CHIPS, 2, ROWS, HEAD), BF16)
    turned = pl.pallas_call(
        layer_kernel,
        name="layer",
        out_shape=jax.ShapeDtypeStruct((own_width, half), BF16),
        in_specs=[SMEM, SMEM, SMEM, ANY, VMEM, ANY, ANY, ANY, ANY, ANY] + [VMEM] * 7,
        out_specs=VMEM,
        scratch_shapes=[
            pltpu.VMEM((2, half, D), BF16),
            pltpu.VMEM((tokens, D), BF16),
            piece,
            piece,
            piece,
            piece,
            pltpu.VMEM((CHIPS, 2, ROWS, 96), BF16),
            pltpu.VMEM((tokens, 256), F32),
            pltpu.VMEM((2, 48, half), F32),
            pltpu.VMEM((48, half), F32),
            pltpu.VMEM((48, half), BF16),
            pltpu.VMEM((PLANES, 48, half), BF16),
            pltpu.VMEM((2, 48, half), BF16),
            pltpu.VMEM((tokens, 2 * HEAD), BF16),
            pltpu.VMEM((tokens, HEAD), BF16),
            pltpu.VMEM((tokens, HEAD), BF16),
            pltpu.VMEM((CHIPS, tokens, HEAD), BF16),
            pltpu.VMEM((CHIPS, tokens, HEAD), BF16),
            pltpu.VMEM((2, 1, tokens), F32),
            pltpu.VMEM((2, 1, tokens), F32),
            pltpu.VMEM((2, HEAD, tokens), F32),
            pltpu.VMEM((2 * HEAD + RANK, tokens), BF16),
            pltpu.VMEM((PLANES, 2 * HEAD + RANK, tokens), BF16),
            pltpu.VMEM((ROWS, 4 * HEAD), BF16),
            piece,
            piece,
            pltpu.VMEM((own_width + RANK, tokens), F32),
            pltpu.VMEM((own_width + RANK, half), BF16),
            pltpu.VMEM((own_width + RANK, half), BF16),
            pltpu.VMEM((8, half), F32),
            pltpu.VMEM((PLANES, 8, half), F32),
            pltpu.VMEM((640, half), F32),
            DMA((9, 20)),
            DMA((9, 24)),
            DMA((8,)),
            DMA((8,)),
            DMA((16,)),
            DMA((20,)),
            DMA((8,)),
            DMA((8,)),
            DMA((13,)),
        ],
        compiler_params=pltpu.CompilerParams(
            collective_id=0, has_side_effects=True, vmem_limit_bytes=60 * 1024 * 1024
        ),
    )(
        prompt_lengths, prompt_adapters, sink_logits, residual, pre_gain, query_weight, key_weight,
        value_weight, adapter_down, output_weight.T, adapter_up_query, adapter_up_key, adapter_up_value,
        adapter_down_out, adapter_up_out.T, post_gain, freq,
    )
    return turned.T


def solution(mesh):
    return jax.shard_map(
        per_device,
        mesh=mesh,
        in_specs=(
            P("wide", None),
            P(),
            P("wide", "narrow"),
            P("wide", "narrow"),
            P("wide", "narrow"),
            P("narrow", "wide"),
            P("wide", "narrow"),
            P(None, "narrow"),
            P(None, "narrow"),
            P(None, "narrow"),
            P("narrow", None),
            P(None, "narrow"),
            P("narrow"),
            P("narrow"),
            P(),
            P(),
        ),
        out_specs=P("wide", "narrow"),
        check_vma=False,
    )
```

time: 156 us -> 127 us (0.81); the launches traced: 156 us -> 125 us
  Pallas kernels: 144 us -> 123 us
  local copies, waits for them, and re-layouts: 10.2 us -> 1.69 us
  starting transfers between devices: 1.56 us -> 0 us
    pallas_call x3 -> x1, Pallas kernels: 144 us -> 123 us  [per_device(): pl.pallas_call(layer_kernel, name='layer', out_shape=jax.ShapeDtypeStruct...]
    broadcast_in_dim x2 -> x0, local copies, waits for them, and re-layouts: 2.57 us -> none  [the longest x1 1.31 us: per_device(): pre_gain[None, :]]
    dynamic_slice x1 -> x0, local copies, waits for them, and re-layouts: 1.89 us -> none  [per_device(): lax.dynamic_slice_in_dim(residual, lax.axis_index('narrow') * own_width,...]
    pallas_call x1 -> x0, local copies, waits for them, and re-layouts: 1.84 us -> none  [per_device(): pl.pallas_call(output_kernel, name='output', out_shape=shape((half, own_w...]
  transfers between devices with their start and end apart: 1 -> 0, of which waited for: 0 -> 0; matrix products, arithmetic and copies ran while one was open for 5% -> 0% of each run, Pallas kernels for 59% -> 0%
where the time goes in v2:
time: 127 us; the launch traced here: 125 us
  Pallas kernels  123 us (97%)
  local copies, waits for them, and re-layouts  1.69 us (1%)
    pallas_call x1, Pallas kernels, per_device(): pl.pallas_call(layer_kernel, name='layer', out_shape=jax.ShapeDtypeStruct...  123 us

profile of v2, /device:TPU:1, one launch (start us, length us, event | category | flops | bytes accessed | tf_op | source)
XLA Modules:
  0.0 124.9 jit_solution(12178564941294643783)
XLA Ops:
  0.0 123.2 %layer.1 = bf16[576,256]{1,0:T(8,128)(2,1)} custom-call(s32[4]{0:T(128)} %lengths.1, s32[4]{0:T(128)} %adapters.1, f32[4]{0:T(128)} %sinks.1, bf16[256,4608]{1,0:T(8,128)(2,1)} %residual.1, bf16[4608]{0:T(1024)(128)(2,1)} %gain.1, bf16[144,512]{1,0:T(8,128)(2,1)} %qw.1, bf16[144,256]{1,0:T(8,128)(2,1)} %kw.1, bf16[144,256]{1,0:T(8,128)(2,1)} %vw.1, ...), custom_call_target="tpu_custom_call" | custom-call | tf_op jit(solution)/shard_map/layer/pallas_call | solution.py:582
  123.3 1.7 %copy.19 = bf16[256,576]{0,1:T(8,128)(2,1)} copy(bf16[256,576]{0,1:T(8,128)(2,1)} %bitcast.3) | data formatting | bytes 589824
